TPU v7x, 32 devices: a whole 2x2x4 slice. The times are simulated.
32 devices in a mesh: wide: 16 (over z, y, x), narrow: 2 (over core).
Axes of the slice: x: 2, y: 2, z: 4, core: 2. Of those that a mesh axis runs over, the one named last changes fastest.
Arguments:
- pressure: float32 [128, 128, 512], P('wide', 'narrow'), may hold values from -6 to 6
Outputs:
- detail_one: float32 [7, 64, 64, 256], P(None, 'wide', 'narrow')
- detail_two: float32 [7, 32, 32, 128], P(None, 'wide', 'narrow')
- detail_three: float32 [7, 16, 16, 64], P(None, 'wide', 'narrow')
- bands_four: float32 [8, 8, 8, 32], P(None, None, 'narrow')
All inputs are finite; a program needn't handle non-finite values.
Results may differ from a plain program's by a relative error of at most 0.00016.
Values sent between devices are 32-bit elements; how exact they have to be, the bound alone decides.
No kernel may reach another device: no remote copies, remote signals or barrier semaphores. Data moves between devices by JAX's collectives and lax.ppermute only.
A program may use at most 64 MiB of HBM per device.

v0:
```python
import jax
import jax.numpy as jnp
from jax import lax
from jax.sharding import PartitionSpec as P

LEVELS = 4
LIFT_ALPHA = -1.586134342
LIFT_BETA = -0.05298011854
LIFT_GAMMA = 0.8829110762
LIFT_DELTA = 0.4435068522
LIFT_ZETA = 1.149604398
LIFT_INVERSE = 1.0 / 1.149604398


def extended(cells, sides, width):
    for axis, dim in sides:
        count = lax.axis_size(axis)
        ends = count - 1
        head = lax.slice_in_dim(cells, 0, width, axis=dim)
        tail = lax.slice_in_dim(cells, cells.shape[dim] - width, cells.shape[dim], axis=dim)
        cells = jnp.concatenate(
            [
                lax.ppermute(tail, axis, [(i, (i + 1) % count) for i in range(ends)]),
                cells,
                lax.ppermute(head, axis, [((i + 1) % count, i) for i in range(ends)]),
            ],
            axis=dim,
        )
    return cells


def shifted(value, axis, steps):
    count = lax.axis_size(axis)
    first, last = (max(0, -steps), min(count, count - steps))
    return lax.ppermute(value, axis, [(source, source + steps) for source in range(first, last)])


def keep_same(piece):
    return piece


def lift_general(volume, along, pull_next, pull_prev, at_first, at_last):
    length = volume.shape[along]
    half = length // 2
    even_part = lax.slice_in_dim(volume, 0, length, 2, along)
    odd_part = lax.slice_in_dim(volume, 1, length, 2, along)

    def next_even(source):
        edge = lax.slice_in_dim(source, half - 1, half, 1, along)
        outer = jnp.where(at_last, edge, pull_next(lax.slice_in_dim(source, 0, 1, 1, along)))
        return jnp.concatenate([lax.slice_in_dim(source, 1, half, 1, along), outer], along)

    def prev_odd(source):
        edge = lax.slice_in_dim(source, 0, 1, 1, along)
        outer = jnp.where(
            at_first, edge, pull_prev(lax.slice_in_dim(source, half - 1, half, 1, along))
        )
        return jnp.concatenate([outer, lax.slice_in_dim(source, 0, half - 1, 1, along)], along)

    odd_part = odd_part + LIFT_ALPHA * (even_part + next_even(even_part))
    even_part = even_part + LIFT_BETA * (prev_odd(odd_part) + odd_part)
    odd_part = odd_part + LIFT_GAMMA * (even_part + next_even(even_part))
    even_part = even_part + LIFT_DELTA * (prev_odd(odd_part) + odd_part)
    return jnp.stack([even_part * LIFT_ZETA, odd_part * LIFT_INVERSE], 0)


def lift_local(volume, along):
    return lift_general(volume, along, keep_same, keep_same, True, True)


def lift_columns(volume):
    width = volume.shape[2]
    unit_matrix = jnp.eye(width, dtype=jnp.float32)
    lift_table = lift_local(unit_matrix, 1)
    return jnp.einsum("zyi,bij->bzyj", volume, lift_table, precision=lax.Precision.HIGHEST)


def lift_widened(widened, along, at_first, at_last):
    total = widened.shape[along]
    left_mirror = jnp.flip(lax.slice_in_dim(widened, 5, 9, 1, along), along)
    right_mirror = jnp.flip(lax.slice_in_dim(widened, total - 9, total - 5, 1, along), along)
    left_part = jnp.where(at_first, left_mirror, lax.slice_in_dim(widened, 0, 4, 1, along))
    right_part = jnp.where(
        at_last, right_mirror, lax.slice_in_dim(widened, total - 4, total, 1, along)
    )
    middle = lax.slice_in_dim(widened, 4, total - 4, 1, along)
    filled = jnp.concatenate([left_part, middle, right_part], along)
    lifted = lift_local(filled, along)
    owned = (total - 8) // 2
    return lax.slice_in_dim(lifted, 2, 2 + owned, 1, along + 1)


def widen_rows(piece):
    return extended(piece, (("narrow", 2),), 4)


def widen_planes(piece):
    return extended(piece, (("wide", 2),), 4)


def pull_next_y(piece):
    return shifted(piece, "narrow", -1)


def pull_prev_y(piece):
    return shifted(piece, "narrow", 1)


def pull_next_z(piece):
    return shifted(piece, "wide", -1)


def pull_prev_z(piece):
    return shifted(piece, "wide", 1)


def per_device(pressure):
    wide_index = lax.axis_index("wide")
    narrow_index = lax.axis_index("narrow")
    wide_count = lax.axis_size("wide")
    wide_first = wide_index == 0
    wide_last = wide_index == wide_count - 1
    narrow_first = narrow_index == 0
    narrow_last = narrow_index == lax.axis_size("narrow") - 1
    volume = pressure
    details = []
    for _ in range(LEVELS - 1):
        planes_here = volume.shape[0]
        x_pair = lift_columns(volume)
        y_pair = lift_widened(widen_rows(x_pair), 2, narrow_first, narrow_last)
        if planes_here >= 4:
            z_pair = lift_widened(widen_planes(y_pair), 2, wide_first, wide_last)
        else:
            z_pair = lift_general(y_pair, 2, pull_next_z, pull_prev_z, wide_first, wide_last)
        band_set = z_pair.reshape((8,) + z_pair.shape[3:])
        details.append(band_set[1:])
        volume = band_set[0]
    whole = lax.all_gather(volume, "wide", axis=0, tiled=True)
    x_pair = lift_columns(whole)
    y_pair = lift_general(x_pair, 2, pull_next_y, pull_prev_y, narrow_first, narrow_last)
    z_pair = lift_local(y_pair, 2)
    last_bands = z_pair.reshape((8,) + z_pair.shape[3:])
    return (details[0], details[1], details[2], last_bands)


def solution(mesh):
    in_specs = (P("wide", "narrow", None),)
    out_specs = (
        P(None, "wide", "narrow", None),
        P(None, "wide", "narrow", None),
        P(None, "wide", "narrow", None),
        P(None, None, "narrow", None),
    )
    return jax.shard_map(
        per_device, mesh=mesh, in_specs=in_specs, out_specs=out_specs, check_vma=False
    )
```

profile of v0, /device:TPU:0, one launch (start us, length us, event | category | flops | bytes accessed | tf_op | source)
XLA Modules:
  0.0 196.4 jit_solution(12183372360742501875)
XLA Ops:
  0.8 19.5 %slice.508 = f32[512,256]{1,0:T(8,128)S(1)} slice(f32[512,512]{1,0:T(8,128)S(1)} %fusion.14), slice={[0:512:1], [1:512:2]} | slice | bytes 1048576 | tf_op jit(solution)/shard_map/slice | solution.py:46
  20.2 19.5 %slice.507 = f32[512,256]{1,0:T(8,128)S(1)} slice(f32[512,512]{1,0:T(8,128)S(1)} %fusion.14), slice={[0:512:1], [0:512:2]} | slice | bytes 1048576 | tf_op jit(solution)/shard_map/slice | solution.py:45
  39.8 0.2 slice.651
  40.2 0.2 fusion.31
  40.6 0.2 slice.655
  40.8 0.2 multiply_bitcast_fusion.2
  41.0 0.2 fusion.37
  41.2 1.9 convolution_bitcast_fusion
  43.1 1.3 collective-permute-start.1
  44.4 3.2 %collective-permute-start = (f32[2,8,4,256]{3,2,1,0:T(4,128)S(1)}, f32[2,8,4,256]{3,2,1,0:T(4,128)S(1)}, u32[]{:S(2)}, u32[]{:S(2)}) collective-permute-start(f32[2,8,4,256]{3,2,1,0:T(4,128)S(1)} %get-tuple-element.40), channel_id=1, source_target_pairs={{0,1},{2,3},{4,5},{6,7},{8,9},{10,11},{12,13},{14,15},{16,17},{18,... | collective-permute-start | bytes 196616 | tf_op jit(solution)/shard_map/ppermute | solution.py:23
  47.7 4.5 %slice.549 = f32[256,128]{1,0:T(8,128)S(1)} slice(f32[256,256]{1,0:T(8,128)S(1)} %fusion.40), slice={[0:256:1], [1:256:2]} | slice | bytes 262144 | tf_op jit(solution)/shard_map/slice | solution.py:46
  52.2 4.5 %slice.548 = f32[256,128]{1,0:T(8,128)S(1)} slice(f32[256,256]{1,0:T(8,128)S(1)} %fusion.40), slice={[0:256:1], [0:256:2]} | slice | bytes 262144 | tf_op jit(solution)/shard_map/slice | solution.py:45
  57.3 0.8 slice.693
  58.0 0.7 slice.692
  58.8 0.6 slice.722
  59.5 0.2 rev.35
  59.9 0.6 slice.521
  60.6 2.2 %slice.522 = f32[2,8,36,256]{3,2,1,0:T(8,128)} slice(f32[2,8,72,256]{3,2,1,0:T(8,128)S(1)} %pad_maximum_fusion.1), slice={[0:2:1], [0:8:1], [1:72:2], [0:256:1]} | slice | bytes 1179648 | tf_op jit(solution)/shard_map/slice | solution.py:46
  62.8 1.0 copy-done.1
  64.2 0.2 multiply_bitcast_fusion.1
  64.4 0.2 fusion.24
  64.6 0.2 fusion.26
  64.8 1.3 collective-permute-start.3
  66.2 5.5 %collective-permute-start.2 = (f32[2,2,4,32,256]{4,3,2,1,0:T(8,128)S(1)}, f32[2,2,4,32,256]{4,3,2,1,0:T(8,128)S(1)}, u32[]{:S(2)}, u32[]{:S(2)}) collective-permute-start(f32[2,2,4,32,256]{4,3,2,1,0:T(8,128)S(1)} %get-tuple-element.37), channel_id=1, source_target_pairs={{0,2},{2,4},{4,6},{6,8},{8,10},{10,12},{12,14},{14,16},{16,18},{18... | collective-permute-start | bytes 1572872 | tf_op jit(solution)/shard_map/ppermute | solution.py:23
  72.0 10.4 %collective-permute-done.3 = f32[2,2,4,32,256]{4,3,2,1,0:T(8,128)S(1)} collective-permute-done((f32[2,2,4,32,256]{4,3,2,1,0:T(8,128)S(1)}, f32[2,2,4,32,256]{4,3,2,1,0:T(8,128)S(1)}, u32[]{:S(2)}, u32[]{:S(2)}) %collective-permute-start.3) | collective-permute-done | bytes 524320 | tf_op jit(solution)/shard_map/ppermute | solution.py:25
  82.5 11.0 %collective-permute-done.2 = f32[2,2,4,32,256]{4,3,2,1,0:T(8,128)S(1)} collective-permute-done((f32[2,2,4,32,256]{4,3,2,1,0:T(8,128)S(1)}, f32[2,2,4,32,256]{4,3,2,1,0:T(8,128)S(1)}, u32[]{:S(2)}, u32[]{:S(2)}) %collective-permute-start.2) | collective-permute-done | bytes 524320 | tf_op jit(solution)/shard_map/ppermute | solution.py:23
  93.5 0.2 pad_maximum_fusion
  94.0 0.3 fusion.4
  94.4 0.3 fusion.6
  94.8 0.3 multiply_bitcast_fusion
  95.2 0.3 fusion.12
  95.7 0.3 convolution_bitcast_fusion.1
  96.0 1.3 collective-permute-start.5
  97.4 3.0 %collective-permute-start.4 = (f32[2,4,4,128]{3,2,1,0:T(4,128)S(1)}, f32[2,4,4,128]{3,2,1,0:T(4,128)S(1)}, u32[]{:S(2)}, u32[]{:S(2)}) collective-permute-start(f32[2,4,4,128]{3,2,1,0:T(4,128)S(1)} %get-tuple-element.46), channel_id=1, source_target_pairs={{0,1},{2,3},{4,5},{6,7},{8,9},{10,11},{12,13},{14,15},{16,17},{18,... | collective-permute-start | bytes 49160 | tf_op jit(solution)/shard_map/ppermute | solution.py:23
  100.5 0.8 collective-permute-done.4
  101.8 1.3 collective-permute-start.6
  103.1 5.0 %collective-permute-start.7 = (f32[2,2,4,16,128]{4,3,2,1,0:T(8,128)S(1)}, f32[2,2,4,16,128]{4,3,2,1,0:T(8,128)S(1)}, u32[]{:S(2)}, u32[]{:S(2)}) collective-permute-start(f32[2,2,4,16,128]{4,3,2,1,0:T(8,128)S(1)} %pad_maximum_fusion.9), channel_id=1, source_target_pairs={{0,2},{2,4},{4,6},{6,8},{8,10},{10,12},{12,14},{14,16},{16,18},{18... | collective-permute-start | bytes 393224 | tf_op jit(solution)/shard_map/ppermute | solution.py:23
  108.1 2.0 %collective-permute-done.6 = f32[2,2,4,16,128]{4,3,2,1,0:T(8,128)S(1)} collective-permute-done((f32[2,2,4,16,128]{4,3,2,1,0:T(8,128)S(1)}, f32[2,2,4,16,128]{4,3,2,1,0:T(8,128)S(1)}, u32[]{:S(2)}, u32[]{:S(2)}) %collective-permute-start.6) | collective-permute-done | bytes 131104 | tf_op jit(solution)/shard_map/ppermute | solution.py:25
  110.2 2.0 %collective-permute-done.7 = f32[2,2,4,16,128]{4,3,2,1,0:T(8,128)S(1)} collective-permute-done((f32[2,2,4,16,128]{4,3,2,1,0:T(8,128)S(1)}, f32[2,2,4,16,128]{4,3,2,1,0:T(8,128)S(1)}, u32[]{:S(2)}, u32[]{:S(2)}) %collective-permute-start.7) | collective-permute-done | bytes 131104 | tf_op jit(solution)/shard_map/ppermute | solution.py:23
  112.7 0.3 convolution_bitcast_fusion.3
  113.0 1.3 collective-permute-start.9
  114.4 3.0 %collective-permute-start.8 = (f32[2,2,4,64]{3,2,1,0:T(4,128)S(1)}, f32[2,2,4,64]{3,2,1,0:T(4,128)S(1)}, u32[]{:S(2)}, u32[]{:S(2)}) collective-permute-start(f32[2,2,4,64]{3,2,1,0:T(4,128)S(1)} %get-tuple-element.50), channel_id=1, source_target_pairs={{0,1},{2,3},{4,5},{6,7},{8,9},{10,11},{12,13},{14,15},{16,17},{18,... | collective-permute-start | bytes 12296 | tf_op jit(solution)/shard_map/ppermute | solution.py:23
  117.5 0.8 collective-permute-done.8
  118.7 1.3 collective-permute-start.10
  120.0 4.7 %collective-permute-done.10 = f32[2,2,1,8,64]{4,3,1,0,2:T(8,128)S(1)} collective-permute-done((f32[2,2,1,8,64]{4,3,1,0,2:T(8,128)S(1)}, f32[2,2,1,8,64]{4,3,1,0,2:T(8,128)S(1)}, u32[]{:S(2)}, u32[]{:S(2)}) %collective-permute-start.10) | collective-permute-done | bytes 8224 | tf_op jit(solution)/shard_map/ppermute | solution.py:35
  124.7 4.8 %collective-permute-start.11 = (f32[2,2,1,8,64]{4,3,1,0,2:T(8,128)S(1)}, f32[2,2,1,8,64]{4,3,1,0,2:T(8,128)S(1)}, u32[]{:S(2)}, u32[]{:S(2)}) collective-permute-start(f32[2,2,1,8,64]{4,3,1,0,2:T(8,128)S(1)} %bitcast.179), channel_id=1, source_target_pairs={{0,2},{2,4},{4,6},{6,8},{8,10},{10,12},{12,14},{14,16},{16,18},{18... | collective-permute-start | bytes 24584 | tf_op jit(solution)/shard_map/ppermute | solution.py:35
  129.6 1.4 collective-permute-done.11
  131.0 1.3 collective-permute-start.12
  132.3 4.6 %collective-permute-done.12 = f32[2,2,1,8,64]{4,3,1,0,2:T(8,128)S(1)} collective-permute-done((f32[2,2,1,8,64]{4,3,1,0,2:T(8,128)S(1)}, f32[2,2,1,8,64]{4,3,1,0,2:T(8,128)S(1)}, u32[]{:S(2)}, u32[]{:S(2)}) %collective-permute-start.12) | collective-permute-done | bytes 8224 | tf_op jit(solution)/shard_map/ppermute | solution.py:35
  136.9 4.8 %collective-permute-start.13 = (f32[2,2,1,8,64]{4,3,1,0,2:T(8,128)S(1)}, f32[2,2,1,8,64]{4,3,1,0,2:T(8,128)S(1)}, u32[]{:S(2)}, u32[]{:S(2)}) collective-permute-start(f32[2,2,1,8,64]{4,3,1,0,2:T(8,128)S(1)} %bitcast.189), channel_id=1, source_target_pairs={{0,2},{2,4},{4,6},{6,8},{8,10},{10,12},{12,14},{14,16},{16,18},{18... | collective-permute-start | bytes 24584 | tf_op jit(solution)/shard_map/ppermute | solution.py:35
  141.8 1.4 collective-permute-done.13
  143.2 38.1 %all-gather = f32[16,1,8,64]{3,2,1,0:T(8,128)S(1)} all-gather(f32[1,1,8,64]{3,2,1,0:T(8,128)S(1)} %slice.748), channel_id=2, replica_groups=mesh['wide'=16,'narrow'=2] {'wide'}, dimensions={0}, use_global_device_ids=true | all-gather | bytes 34816 | tf_op jit(solution)/shard_map/all_gather | solution.py:138
  181.3 0.3 convolution_bitcast_fusion.2
  181.6 1.3 collective-permute-start.14
  183.0 1.8 collective-permute-done.14
  184.8 2.1 %collective-permute-start.15 = (f32[2,16,1,32]{3,1,2,0:T(8,128)S(1)}, f32[2,16,1,32]{3,1,2,0:T(8,128)S(1)}, u32[]{:S(2)}, u32[]{:S(2)}) collective-permute-start(f32[2,16,1,32]{3,1,2,0:T(8,128)S(1)} %slice.753), channel_id=1, source_target_pairs={{0,1},{2,3},{4,5},{6,7},{8,9},{10,11},{12,13},{14,15},{16,17},{18,... | collective-permute-start | bytes 12296 | tf_op jit(solution)/shard_map/ppermute | solution.py:35
  186.8 0.8 collective-permute-done.15
  187.7 1.3 collective-permute-start.16
  189.0 1.8 collective-permute-done.16
  190.8 2.1 %collective-permute-start.17 = (f32[2,16,1,32]{3,1,2,0:T(8,128)S(1)}, f32[2,16,1,32]{3,1,2,0:T(8,128)S(1)}, u32[]{:S(2)}, u32[]{:S(2)}) collective-permute-start(f32[2,16,1,32]{3,1,2,0:T(8,128)S(1)} %slice.759), channel_id=1, source_target_pairs={{0,1},{2,3},{4,5},{6,7},{8,9},{10,11},{12,13},{14,15},{16,17},{18,... | collective-permute-start | bytes 12296 | tf_op jit(solution)/shard_map/ppermute | solution.py:35
  192.9 1.0 slice.687
  193.9 0.7 slice.717
  194.5 0.6 slice.739
  195.7 0.7 copy.29
  (179 shorter events, 4.8 us)
Async XLA Ops:
  0.6 40.6 %copy-start = (f32[8,64,512]{2,1,0:T(8,128)S(1)}, f32[8,64,512]{2,1,0:T(8,128)}, u32[]{:S(2)}) copy-start(f32[8,64,512]{2,1,0:T(8,128)} %param.1) | copy-start | bytes 3145732
  43.1 16.5 %collective-permute-start.1 = (f32[2,8,4,256]{3,2,1,0:T(4,128)S(1)}, f32[2,8,4,256]{3,2,1,0:T(4,128)S(1)}, u32[]{:S(2)}, u32[]{:S(2)}) collective-permute-start(f32[2,8,4,256]{3,2,1,0:T(4,128)S(1)} %get-tuple-element.41), channel_id=1, source_target_pairs={{1,0},{3,2},{5,4},{7,6},{9,8},{11,10},{13,12},{15,14},{17,16},{19,... | collective-permute-start | bytes 196616 | tf_op jit(solution)/shard_map/ppermute | solution.py:25
  44.4 15.3 %collective-permute-start = (f32[2,8,4,256]{3,2,1,0:T(4,128)S(1)}, f32[2,8,4,256]{3,2,1,0:T(4,128)S(1)}, u32[]{:S(2)}, u32[]{:S(2)}) collective-permute-start(f32[2,8,4,256]{3,2,1,0:T(4,128)S(1)} %get-tuple-element.40), channel_id=1, source_target_pairs={{0,1},{2,3},{4,5},{6,7},{8,9},{10,11},{12,13},{14,15},{16,17},{18,... | collective-permute-start | bytes 196616 | tf_op jit(solution)/shard_map/ppermute | solution.py:23
  57.0 2.8 %copy-start.6 = (f32[128,64]{0,1:T(8,128)}, f32[128,64]{0,1:T(8,128)S(1)}, u32[]{:S(2)}) copy-start(f32[128,64]{0,1:T(8,128)S(1)} %fusion.97) | copy-start | bytes 98308
  57.3 2.5 %copy-start.2 = (f32[128,64]{0,1:T(8,128)}, f32[128,64]{0,1:T(8,128)S(1)}, u32[]{:S(2)}) copy-start(f32[128,64]{0,1:T(8,128)S(1)} %fusion.99) | copy-start | bytes 98308
  62.8 1.1 copy-start.1
  64.6 1.5 copy-start.4
  64.6 1.5 copy-start.5
  64.8 17.6 %collective-permute-start.3 = (f32[2,2,4,32,256]{4,3,2,1,0:T(8,128)S(1)}, f32[2,2,4,32,256]{4,3,2,1,0:T(8,128)S(1)}, u32[]{:S(2)}, u32[]{:S(2)}) collective-permute-start(f32[2,2,4,32,256]{4,3,2,1,0:T(8,128)S(1)} %get-tuple-element.38), channel_id=1, source_target_pairs={{2,0},{4,2},{6,4},{8,6},{10,8},{12,10},{14,12},{16,14},{18,16},{20... | collective-permute-start | bytes 1572872 | tf_op jit(solution)/shard_map/ppermute | solution.py:25
  66.2 27.2 %collective-permute-start.2 = (f32[2,2,4,32,256]{4,3,2,1,0:T(8,128)S(1)}, f32[2,2,4,32,256]{4,3,2,1,0:T(8,128)S(1)}, u32[]{:S(2)}, u32[]{:S(2)}) collective-permute-start(f32[2,2,4,32,256]{4,3,2,1,0:T(8,128)S(1)} %get-tuple-element.37), channel_id=1, source_target_pairs={{0,2},{2,4},{4,6},{6,8},{8,10},{10,12},{12,14},{14,16},{16,18},{18... | collective-permute-start | bytes 1572872 | tf_op jit(solution)/shard_map/ppermute | solution.py:23
  95.5 1.8 copy-start.3
  95.6 1.8 copy-start.7
  95.6 1.8 copy-start.8
  96.0 4.5 %collective-permute-start.5 = (f32[2,4,4,128]{3,2,1,0:T(4,128)S(1)}, f32[2,4,4,128]{3,2,1,0:T(4,128)S(1)}, u32[]{:S(2)}, u32[]{:S(2)}) collective-permute-start(f32[2,4,4,128]{3,2,1,0:T(4,128)S(1)} %get-tuple-element.47), channel_id=1, source_target_pairs={{1,0},{3,2},{5,4},{7,6},{9,8},{11,10},{13,12},{15,14},{17,16},{19,... | collective-permute-start | bytes 49160 | tf_op jit(solution)/shard_map/ppermute | solution.py:25
  97.4 3.9 %collective-permute-start.4 = (f32[2,4,4,128]{3,2,1,0:T(4,128)S(1)}, f32[2,4,4,128]{3,2,1,0:T(4,128)S(1)}, u32[]{:S(2)}, u32[]{:S(2)}) collective-permute-start(f32[2,4,4,128]{3,2,1,0:T(4,128)S(1)} %get-tuple-element.46), channel_id=1, source_target_pairs={{0,1},{2,3},{4,5},{6,7},{8,9},{10,11},{12,13},{14,15},{16,17},{18,... | collective-permute-start | bytes 49160 | tf_op jit(solution)/shard_map/ppermute | solution.py:23
  101.8 8.4 %collective-permute-start.6 = (f32[2,2,4,16,128]{4,3,2,1,0:T(8,128)S(1)}, f32[2,2,4,16,128]{4,3,2,1,0:T(8,128)S(1)}, u32[]{:S(2)}, u32[]{:S(2)}) collective-permute-start(f32[2,2,4,16,128]{4,3,2,1,0:T(8,128)S(1)} %pad_maximum_fusion.9), channel_id=1, source_target_pairs={{2,0},{4,2},{6,4},{8,6},{10,8},{12,10},{14,12},{16,14},{18,16},{20... | collective-permute-start | bytes 393224 | tf_op jit(solution)/shard_map/ppermute | solution.py:25
  103.1 9.1 %collective-permute-start.7 = (f32[2,2,4,16,128]{4,3,2,1,0:T(8,128)S(1)}, f32[2,2,4,16,128]{4,3,2,1,0:T(8,128)S(1)}, u32[]{:S(2)}, u32[]{:S(2)}) collective-permute-start(f32[2,2,4,16,128]{4,3,2,1,0:T(8,128)S(1)} %pad_maximum_fusion.9), channel_id=1, source_target_pairs={{0,2},{2,4},{4,6},{6,8},{8,10},{10,12},{12,14},{14,16},{16,18},{18... | collective-permute-start | bytes 393224 | tf_op jit(solution)/shard_map/ppermute | solution.py:23
  113.0 4.5 %collective-permute-start.9 = (f32[2,2,4,64]{3,2,1,0:T(4,128)S(1)}, f32[2,2,4,64]{3,2,1,0:T(4,128)S(1)}, u32[]{:S(2)}, u32[]{:S(2)}) collective-permute-start(f32[2,2,4,64]{3,2,1,0:T(4,128)S(1)} %get-tuple-element.51), channel_id=1, source_target_pairs={{1,0},{3,2},{5,4},{7,6},{9,8},{11,10},{13,12},{15,14},{17,16},{19,... | collective-permute-start | bytes 12296 | tf_op jit(solution)/shard_map/ppermute | solution.py:25
  114.4 3.8 %collective-permute-start.8 = (f32[2,2,4,64]{3,2,1,0:T(4,128)S(1)}, f32[2,2,4,64]{3,2,1,0:T(4,128)S(1)}, u32[]{:S(2)}, u32[]{:S(2)}) collective-permute-start(f32[2,2,4,64]{3,2,1,0:T(4,128)S(1)} %get-tuple-element.50), channel_id=1, source_target_pairs={{0,1},{2,3},{4,5},{6,7},{8,9},{10,11},{12,13},{14,15},{16,17},{18,... | collective-permute-start | bytes 12296 | tf_op jit(solution)/shard_map/ppermute | solution.py:23
  118.7 6.1 %collective-permute-start.10 = (f32[2,2,1,8,64]{4,3,1,0,2:T(8,128)S(1)}, f32[2,2,1,8,64]{4,3,1,0,2:T(8,128)S(1)}, u32[]{:S(2)}, u32[]{:S(2)}) collective-permute-start(f32[2,2,1,8,64]{4,3,1,0,2:T(8,128)S(1)} %maximum_bitcast_fusion.8), channel_id=1, source_target_pairs={{2,0},{4,2},{6,4},{8,6},{10,8},{12,10},{14,12},{16,14},{18,16},{20... | collective-permute-start | bytes 24584 | tf_op jit(solution)/shard_map/ppermute | solution.py:35
  124.7 6.3 %collective-permute-start.11 = (f32[2,2,1,8,64]{4,3,1,0,2:T(8,128)S(1)}, f32[2,2,1,8,64]{4,3,1,0,2:T(8,128)S(1)}, u32[]{:S(2)}, u32[]{:S(2)}) collective-permute-start(f32[2,2,1,8,64]{4,3,1,0,2:T(8,128)S(1)} %bitcast.179), channel_id=1, source_target_pairs={{0,2},{2,4},{4,6},{6,8},{8,10},{10,12},{12,14},{14,16},{16,18},{18... | collective-permute-start | bytes 24584 | tf_op jit(solution)/shard_map/ppermute | solution.py:35
  131.0 5.9 %collective-permute-start.12 = (f32[2,2,1,8,64]{4,3,1,0,2:T(8,128)S(1)}, f32[2,2,1,8,64]{4,3,1,0,2:T(8,128)S(1)}, u32[]{:S(2)}, u32[]{:S(2)}) collective-permute-start(f32[2,2,1,8,64]{4,3,1,0,2:T(8,128)S(1)} %fusion.123), channel_id=1, source_target_pairs={{2,0},{4,2},{6,4},{8,6},{10,8},{12,10},{14,12},{16,14},{18,16},{20... | collective-permute-start | bytes 24584 | tf_op jit(solution)/shard_map/ppermute | solution.py:35
  136.9 6.3 %collective-permute-start.13 = (f32[2,2,1,8,64]{4,3,1,0,2:T(8,128)S(1)}, f32[2,2,1,8,64]{4,3,1,0,2:T(8,128)S(1)}, u32[]{:S(2)}, u32[]{:S(2)}) collective-permute-start(f32[2,2,1,8,64]{4,3,1,0,2:T(8,128)S(1)} %bitcast.189), channel_id=1, source_target_pairs={{0,2},{2,4},{4,6},{6,8},{8,10},{10,12},{12,14},{14,16},{16,18},{18... | collective-permute-start | bytes 24584 | tf_op jit(solution)/shard_map/ppermute | solution.py:35
  181.6 3.1 %collective-permute-start.14 = (f32[2,16,1,32]{3,1,2,0:T(8,128)S(1)}, f32[2,16,1,32]{3,1,2,0:T(8,128)S(1)}, u32[]{:S(2)}, u32[]{:S(2)}) collective-permute-start(f32[2,16,1,32]{3,1,2,0:T(8,128)S(1)} %slice.751), channel_id=1, source_target_pairs={{1,0},{3,2},{5,4},{7,6},{9,8},{11,10},{13,12},{15,14},{17,16},{19,... | collective-permute-start | bytes 12296 | tf_op jit(solution)/shard_map/ppermute | solution.py:35
  184.8 2.9 %collective-permute-start.15 = (f32[2,16,1,32]{3,1,2,0:T(8,128)S(1)}, f32[2,16,1,32]{3,1,2,0:T(8,128)S(1)}, u32[]{:S(2)}, u32[]{:S(2)}) collective-permute-start(f32[2,16,1,32]{3,1,2,0:T(8,128)S(1)} %slice.753), channel_id=1, source_target_pairs={{0,1},{2,3},{4,5},{6,7},{8,9},{10,11},{12,13},{14,15},{16,17},{18,... | collective-permute-start | bytes 12296 | tf_op jit(solution)/shard_map/ppermute | solution.py:35
  187.7 3.1 %collective-permute-start.16 = (f32[2,16,1,32]{3,1,2,0:T(8,128)S(1)}, f32[2,16,1,32]{3,1,2,0:T(8,128)S(1)}, u32[]{:S(2)}, u32[]{:S(2)}) collective-permute-start(f32[2,16,1,32]{3,1,2,0:T(8,128)S(1)} %slice.757), channel_id=1, source_target_pairs={{1,0},{3,2},{5,4},{7,6},{9,8},{11,10},{13,12},{15,14},{17,16},{19,... | collective-permute-start | bytes 12296 | tf_op jit(solution)/shard_map/ppermute | solution.py:35
  190.8 4.3 %collective-permute-start.17 = (f32[2,16,1,32]{3,1,2,0:T(8,128)S(1)}, f32[2,16,1,32]{3,1,2,0:T(8,128)S(1)}, u32[]{:S(2)}, u32[]{:S(2)}) collective-permute-start(f32[2,16,1,32]{3,1,2,0:T(8,128)S(1)} %slice.759), channel_id=1, source_target_pairs={{0,1},{2,3},{4,5},{6,7},{8,9},{10,11},{12,13},{14,15},{16,17},{18,... | collective-permute-start | bytes 12296 | tf_op jit(solution)/shard_map/ppermute | solution.py:35
where the time goes:
time: 197 us; the launch traced here: 196 us
  local copies, waits for them, and re-layouts  59.7 us (30%)
  starting transfers between devices  45.2 us (23%)
  waiting for transfers between devices  43.5 us (22%)
  blocking collectives  38.1 us (19%)
  other arithmetic  5.06 us (3%)
  matrix products  2.78 us (1%)
  between operations  2.1 us (1%)
    all_gather x1, blocking collectives, per_device(): whole = lax.all_gather(volume, 'wide', axis=0, tiled=True)  38.1 us
    slice x8, local copies, waits for them, and re-layouts, lift_general(): odd_part = lax.slice_in_dim(volume, 1, length, 2, along)  26.5 us
    slice x11, local copies, waits for them, and re-layouts, lift_general(): even_part = lax.slice_in_dim(volume, 0, length, 2, along)  25.1 us
    ppermute x5, starting transfers between devices, extended(): lax.ppermute(tail, axis, [(i, (i + 1) % count) for i in range(ends)])  19.8 us
    ppermute x8, starting transfers between devices, shifted(): lax.ppermute(value, axis, [(source, source + steps) for source in range(f...  18.9 us
    ppermute x8, waiting for transfers between devices, shifted(): lax.ppermute(value, axis, [(source, source + steps) for source in range(f...  16.5 us
    ppermute x5, waiting for transfers between devices, extended(): lax.ppermute(tail, axis, [(i, (i + 1) % count) for i in range(ends)])  14.6 us
    ppermute x5, waiting for transfers between devices, extended(): lax.ppermute(head, axis, [((i + 1) % count, i) for i in range(ends)])  12.5 us
  transfers between devices with their start and end apart: 18, of which 13 were waited for; matrix products, arithmetic and copies ran while one was open for 8% of the time, Pallas kernels for 0%

commit v1 on v0

--- a/solution.py
+++ b/solution.py
@@ -10,6 +10,28 @@
 LIFT_DELTA = 0.4435068522
 LIFT_ZETA = 1.149604398
 LIFT_INVERSE = 1.0 / 1.149604398
+
+
+def in_order(tiles, dim):
+    tiles = jnp.moveaxis(tiles, 0, dim)
+    shape = tiles.shape
+    return tiles.reshape(*shape[:dim], shape[dim] * shape[dim + 1], *shape[dim + 2 :])
+
+
+def collect(x, axis, dim):
+    count = lax.axis_size(axis)
+    pairs = [(i, (i + 1) % count) for i in range(count)]
+    back = [(b, a) for a, b in pairs]
+    lower, upper = ([], [])
+    for lap in range(count - 1):
+        if lap % 2 == 0:
+            lower.append(lax.ppermute(lower[-1] if lower else x, axis, pairs))
+        else:
+            upper.append(lax.ppermute(upper[-1] if upper else x, axis, back))
+    pieces = jnp.stack([*lower[::-1], x, *upper])
+    shift = lax.axis_index(axis) - len(lower)
+    pieces = pieces[(jnp.arange(count) - shift) % count]
+    return in_order(pieces, dim)
 
 
 def extended(cells, sides, width):
@@ -135,7 +157,7 @@
         band_set = z_pair.reshape((8,) + z_pair.shape[3:])
         details.append(band_set[1:])
         volume = band_set[0]
-    whole = lax.all_gather(volume, "wide", axis=0, tiled=True)
+    whole = collect(volume, "wide", 0)
     x_pair = lift_columns(whole)
     y_pair = lift_general(x_pair, 2, pull_next_y, pull_prev_y, narrow_first, narrow_last)
     z_pair = lift_local(y_pair, 2)

time: 197 us -> 217 us (1.10)
  starting transfers between devices: 45.2 us -> 87.4 us
  blocking collectives: 38.1 us -> 0 us
  waiting for transfers between devices: 43.5 us -> 58.8 us
    ppermute x0 -> x15, starting transfers between devices: none -> 42.2 us  [the longest x7 39.9 us: collect(): upper.append(lax.ppermute(upper[-1] if upper else x, axis, back))]
    all_gather x1 -> x0, blocking collectives: 38.1 us -> none  [per_device(): whole = lax.all_gather(volume, 'wide', axis=0, tiled=True)]
    ppermute x0 -> x15, waiting for transfers between devices: none -> 15.2 us  [the longest x8 15.2 us: collect(): lower.append(lax.ppermute(lower[-1] if lower else x, axis, pairs))]
  transfers between devices with their start and end apart: 18 -> 33, of which waited for: 13 -> 21; matrix products, arithmetic and copies ran while one was open for 8% -> 7% of each run, Pallas kernels for 0% -> 0%
where the time goes in v1:
time: 217 us
  starting transfers between devices  87.4 us (40%)
  local copies, waits for them, and re-layouts  60.3 us (28%)
  waiting for transfers between devices  58.8 us (27%)
  other arithmetic  5.07 us (2%)
  matrix products  2.78 us (1%)
  between operations  2.27 us (1%)
    ppermute x7, starting transfers between devices, collect(): upper.append(lax.ppermute(upper[-1] if upper else x, axis, back))  39.9 us
    slice x8, local copies, waits for them, and re-layouts, lift_general(): odd_part = lax.slice_in_dim(volume, 1, length, 2, along)  26.5 us
    slice x11, local copies, waits for them, and re-layouts, lift_general(): even_part = lax.slice_in_dim(volume, 0, length, 2, along)  25.1 us
    ppermute x5, starting transfers between devices, extended(): lax.ppermute(tail, axis, [(i, (i + 1) % count) for i in range(ends)])  19.8 us
    ppermute x8, starting transfers between devices, shifted(): lax.ppermute(value, axis, [(source, source + steps) for source in range(f...  18.9 us
    ppermute x8, waiting for transfers between devices, shifted(): lax.ppermute(value, axis, [(source, source + steps) for source in range(f...  16.6 us
    ppermute x8, waiting for transfers between devices, collect(): lower.append(lax.ppermute(lower[-1] if lower else x, axis, pairs))  15.2 us
    ppermute x5, waiting for transfers between devices, extended(): lax.ppermute(tail, axis, [(i, (i + 1) % count) for i in range(ends)])  14.6 us
  transfers between devices with their start and end apart: 33, of which 21 were waited for; matrix products, arithmetic and copies ran while one was open for 7% of the time, Pallas kernels for 0%

profile of v1, /device:TPU:0, one launch (start us, length us, event | category | flops | bytes accessed | tf_op | source)
XLA Modules:
  0.0 216.7 jit_solution(10351238507695750786)
XLA Ops:
  0.8 19.5 %slice.508 = f32[512,256]{1,0:T(8,128)S(1)} slice(f32[512,512]{1,0:T(8,128)S(1)} %fusion.14), slice={[0:512:1], [1:512:2]} | slice | bytes 1048576 | tf_op jit(solution)/shard_map/slice | solution.py:68
  20.2 19.5 %slice.507 = f32[512,256]{1,0:T(8,128)S(1)} slice(f32[512,512]{1,0:T(8,128)S(1)} %fusion.14), slice={[0:512:1], [0:512:2]} | slice | bytes 1048576 | tf_op jit(solution)/shard_map/slice | solution.py:67
  41.2 1.9 convolution_bitcast_fusion
  43.1 1.3 collective-permute-start.1
  44.4 3.2 %collective-permute-start = (f32[2,8,4,256]{3,2,1,0:T(4,128)S(1)}, f32[2,8,4,256]{3,2,1,0:T(4,128)S(1)}, u32[]{:S(2)}, u32[]{:S(2)}) collective-permute-start(f32[2,8,4,256]{3,2,1,0:T(4,128)S(1)} %get-tuple-element.40), channel_id=1, source_target_pairs={{0,1},{2,3},{4,5},{6,7},{8,9},{10,11},{12,13},{14,15},{16,17},{18,... | collective-permute-start | bytes 196616 | tf_op jit(solution)/shard_map/ppermute | solution.py:45
  47.7 4.5 %slice.549 = f32[256,128]{1,0:T(8,128)S(1)} slice(f32[256,256]{1,0:T(8,128)S(1)} %fusion.40), slice={[0:256:1], [1:256:2]} | slice | bytes 262144 | tf_op jit(solution)/shard_map/slice | solution.py:68
  52.2 4.5 %slice.548 = f32[256,128]{1,0:T(8,128)S(1)} slice(f32[256,256]{1,0:T(8,128)S(1)} %fusion.40), slice={[0:256:1], [0:256:2]} | slice | bytes 262144 | tf_op jit(solution)/shard_map/slice | solution.py:67
  57.3 0.8 slice.695
  58.0 0.8 slice.694
  58.8 0.6 slice.724
  59.9 0.6 slice.521
  60.6 2.2 %slice.522 = f32[2,8,36,256]{3,2,1,0:T(8,128)} slice(f32[2,8,72,256]{3,2,1,0:T(8,128)S(1)} %pad_maximum_fusion.1), slice={[0:2:1], [0:8:1], [1:72:2], [0:256:1]} | slice | bytes 1179648 | tf_op jit(solution)/shard_map/slice | solution.py:68
  62.9 1.0 copy-done.1
  64.8 1.3 collective-permute-start.3
  66.2 5.5 %collective-permute-start.2 = (f32[2,2,4,32,256]{4,3,2,1,0:T(8,128)S(1)}, f32[2,2,4,32,256]{4,3,2,1,0:T(8,128)S(1)}, u32[]{:S(2)}, u32[]{:S(2)}) collective-permute-start(f32[2,2,4,32,256]{4,3,2,1,0:T(8,128)S(1)} %get-tuple-element.37), channel_id=1, source_target_pairs={{0,2},{2,4},{4,6},{6,8},{8,10},{10,12},{12,14},{14,16},{16,18},{18... | collective-permute-start | bytes 1572872 | tf_op jit(solution)/shard_map/ppermute | solution.py:45
  72.0 10.4 %collective-permute-done.3 = f32[2,2,4,32,256]{4,3,2,1,0:T(8,128)S(1)} collective-permute-done((f32[2,2,4,32,256]{4,3,2,1,0:T(8,128)S(1)}, f32[2,2,4,32,256]{4,3,2,1,0:T(8,128)S(1)}, u32[]{:S(2)}, u32[]{:S(2)}) %collective-permute-start.3) | collective-permute-done | bytes 524320 | tf_op jit(solution)/shard_map/ppermute | solution.py:47
  82.5 11.0 %collective-permute-done.2 = f32[2,2,4,32,256]{4,3,2,1,0:T(8,128)S(1)} collective-permute-done((f32[2,2,4,32,256]{4,3,2,1,0:T(8,128)S(1)}, f32[2,2,4,32,256]{4,3,2,1,0:T(8,128)S(1)}, u32[]{:S(2)}, u32[]{:S(2)}) %collective-permute-start.2) | collective-permute-done | bytes 524320 | tf_op jit(solution)/shard_map/ppermute | solution.py:45
  94.8 0.3 multiply_bitcast_fusion
  96.0 1.3 collective-permute-start.5
  97.5 3.0 %collective-permute-start.4 = (f32[2,4,4,128]{3,2,1,0:T(4,128)S(1)}, f32[2,4,4,128]{3,2,1,0:T(4,128)S(1)}, u32[]{:S(2)}, u32[]{:S(2)}) collective-permute-start(f32[2,4,4,128]{3,2,1,0:T(4,128)S(1)} %get-tuple-element.46), channel_id=1, source_target_pairs={{0,1},{2,3},{4,5},{6,7},{8,9},{10,11},{12,13},{14,15},{16,17},{18,... | collective-permute-start | bytes 49160 | tf_op jit(solution)/shard_map/ppermute | solution.py:45
  100.5 0.8 collective-permute-done.4
  101.8 1.3 collective-permute-start.6
  103.1 5.0 %collective-permute-start.7 = (f32[2,2,4,16,128]{4,3,2,1,0:T(8,128)S(1)}, f32[2,2,4,16,128]{4,3,2,1,0:T(8,128)S(1)}, u32[]{:S(2)}, u32[]{:S(2)}) collective-permute-start(f32[2,2,4,16,128]{4,3,2,1,0:T(8,128)S(1)} %pad_maximum_fusion.9), channel_id=1, source_target_pairs={{0,2},{2,4},{4,6},{6,8},{8,10},{10,12},{12,14},{14,16},{16,18},{18... | collective-permute-start | bytes 393224 | tf_op jit(solution)/shard_map/ppermute | solution.py:45
  108.2 2.0 collective-permute-done.6
  110.2 2.0 collective-permute-done.7
  113.0 1.3 collective-permute-start.9
  114.4 3.0 %collective-permute-start.8 = (f32[2,2,4,64]{3,2,1,0:T(4,128)S(1)}, f32[2,2,4,64]{3,2,1,0:T(4,128)S(1)}, u32[]{:S(2)}, u32[]{:S(2)}) collective-permute-start(f32[2,2,4,64]{3,2,1,0:T(4,128)S(1)} %get-tuple-element.50), channel_id=1, source_target_pairs={{0,1},{2,3},{4,5},{6,7},{8,9},{10,11},{12,13},{14,15},{16,17},{18,... | collective-permute-start | bytes 12296 | tf_op jit(solution)/shard_map/ppermute | solution.py:45
  117.4 0.8 collective-permute-done.8
  118.6 1.3 collective-permute-start.10
  119.9 4.8 %collective-permute-done.10 = f32[2,2,1,8,64]{4,3,1,0,2:T(8,128)S(1)} collective-permute-done((f32[2,2,1,8,64]{4,3,1,0,2:T(8,128)S(1)}, f32[2,2,1,8,64]{4,3,1,0,2:T(8,128)S(1)}, u32[]{:S(2)}, u32[]{:S(2)}) %collective-permute-start.10) | collective-permute-done | bytes 8224 | tf_op jit(solution)/shard_map/ppermute | solution.py:57
  124.7 4.8 %collective-permute-start.11 = (f32[2,2,1,8,64]{4,3,1,0,2:T(8,128)S(1)}, f32[2,2,1,8,64]{4,3,1,0,2:T(8,128)S(1)}, u32[]{:S(2)}, u32[]{:S(2)}) collective-permute-start(f32[2,2,1,8,64]{4,3,1,0,2:T(8,128)S(1)} %bitcast.246), channel_id=1, source_target_pairs={{0,2},{2,4},{4,6},{6,8},{8,10},{10,12},{12,14},{14,16},{16,18},{18... | collective-permute-start | bytes 24584 | tf_op jit(solution)/shard_map/ppermute | solution.py:57
  129.5 1.4 collective-permute-done.11
  131.0 1.3 collective-permute-start.12
  132.2 4.6 %collective-permute-done.12 = f32[2,2,1,8,64]{4,3,1,0,2:T(8,128)S(1)} collective-permute-done((f32[2,2,1,8,64]{4,3,1,0,2:T(8,128)S(1)}, f32[2,2,1,8,64]{4,3,1,0,2:T(8,128)S(1)}, u32[]{:S(2)}, u32[]{:S(2)}) %collective-permute-start.12) | collective-permute-done | bytes 8224 | tf_op jit(solution)/shard_map/ppermute | solution.py:57
  136.9 4.8 %collective-permute-start.13 = (f32[2,2,1,8,64]{4,3,1,0,2:T(8,128)S(1)}, f32[2,2,1,8,64]{4,3,1,0,2:T(8,128)S(1)}, u32[]{:S(2)}, u32[]{:S(2)}) collective-permute-start(f32[2,2,1,8,64]{4,3,1,0,2:T(8,128)S(1)} %bitcast.255), channel_id=1, source_target_pairs={{0,2},{2,4},{4,6},{6,8},{8,10},{10,12},{12,14},{14,16},{16,18},{18... | collective-permute-start | bytes 24584 | tf_op jit(solution)/shard_map/ppermute | solution.py:57
  141.7 1.4 collective-permute-done.13
  143.2 2.4 %collective-permute-start.14 = (f32[1,8,64]{2,1,0:T(8,128)S(1)}, f32[1,8,64]{2,1,0:T(8,128)S(1)}, u32[]{:S(2)}, u32[]{:S(2)}) collective-permute-start(f32[1,8,64]{2,1,0:T(8,128)S(1)} %slice_bitcast_fusion.4), channel_id=1, source_target_pairs={{0,2},{2,4},{4,6},{6,8},{8,10},{10,12},{12,14},{14,16},{16,18},{18... | collective-permute-start | bytes 6152 | tf_op jit(solution)/shard_map/ppermute | solution.py:28
  145.5 4.9 %collective-permute-done.14 = f32[1,8,64]{2,1,0:T(8,128)S(1)} collective-permute-done((f32[1,8,64]{2,1,0:T(8,128)S(1)}, f32[1,8,64]{2,1,0:T(8,128)S(1)}, u32[]{:S(2)}, u32[]{:S(2)}) %collective-permute-start.14) | collective-permute-done | bytes 2080 | tf_op jit(solution)/shard_map/ppermute | solution.py:28
  150.5 5.7 %collective-permute-start.22 = (f32[1,8,64]{2,1,0:T(8,128)S(1)}, f32[1,8,64]{2,1,0:T(8,128)S(1)}, u32[]{:S(2)}, u32[]{:S(2)}) collective-permute-start(f32[1,8,64]{2,1,0:T(8,128)S(1)} %slice_bitcast_fusion.4), channel_id=1, source_target_pairs={{2,0},{4,2},{6,4},{8,6},{10,8},{12,10},{14,12},{16,14},{18,16},{20... | collective-permute-start | bytes 6152 | tf_op jit(solution)/shard_map/ppermute | solution.py:30
  156.1 1.5 collective-permute-done.15
  157.7 5.7 %collective-permute-start.23 = (f32[1,8,64]{2,1,0:T(8,128)S(1)}, f32[1,8,64]{2,1,0:T(8,128)S(1)}, u32[]{:S(2)}, u32[]{:S(2)}) collective-permute-start(f32[1,8,64]{2,1,0:T(8,128)S(1)} %collective-permute-done.22), channel_id=1, source_target_pairs={{2,0},{4,2},{6,4},{8,6},{10,8},{12,10},{14,12},{16,14},{18,16},{20... | collective-permute-start | bytes 6152 | tf_op jit(solution)/shard_map/ppermute | solution.py:30
  163.3 1.5 collective-permute-done.16
  164.9 5.7 %collective-permute-start.24 = (f32[1,8,64]{2,1,0:T(8,128)S(1)}, f32[1,8,64]{2,1,0:T(8,128)S(1)}, u32[]{:S(2)}, u32[]{:S(2)}) collective-permute-start(f32[1,8,64]{2,1,0:T(8,128)S(1)} %collective-permute-done.23), channel_id=1, source_target_pairs={{2,0},{4,2},{6,4},{8,6},{10,8},{12,10},{14,12},{16,14},{18,16},{20... | collective-permute-start | bytes 6152 | tf_op jit(solution)/shard_map/ppermute | solution.py:30
  170.6 1.5 collective-permute-done.17
  172.1 5.7 %collective-permute-start.25 = (f32[1,8,64]{2,1,0:T(8,128)S(1)}, f32[1,8,64]{2,1,0:T(8,128)S(1)}, u32[]{:S(2)}, u32[]{:S(2)}) collective-permute-start(f32[1,8,64]{2,1,0:T(8,128)S(1)} %collective-permute-done.24), channel_id=1, source_target_pairs={{2,0},{4,2},{6,4},{8,6},{10,8},{12,10},{14,12},{16,14},{18,16},{20... | collective-permute-start | bytes 6152 | tf_op jit(solution)/shard_map/ppermute | solution.py:30
  177.8 1.5 collective-permute-done.18
  179.3 5.7 %collective-permute-start.26 = (f32[1,8,64]{2,1,0:T(8,128)S(1)}, f32[1,8,64]{2,1,0:T(8,128)S(1)}, u32[]{:S(2)}, u32[]{:S(2)}) collective-permute-start(f32[1,8,64]{2,1,0:T(8,128)S(1)} %collective-permute-done.25), channel_id=1, source_target_pairs={{2,0},{4,2},{6,4},{8,6},{10,8},{12,10},{14,12},{16,14},{18,16},{20... | collective-permute-start | bytes 6152 | tf_op jit(solution)/shard_map/ppermute | solution.py:30
  185.0 1.5 collective-permute-done.19
  186.5 5.7 %collective-permute-start.27 = (f32[1,8,64]{2,1,0:T(8,128)S(1)}, f32[1,8,64]{2,1,0:T(8,128)S(1)}, u32[]{:S(2)}, u32[]{:S(2)}) collective-permute-start(f32[1,8,64]{2,1,0:T(8,128)S(1)} %collective-permute-done.26), channel_id=1, source_target_pairs={{2,0},{4,2},{6,4},{8,6},{10,8},{12,10},{14,12},{16,14},{18,16},{20... | collective-permute-start | bytes 6152 | tf_op jit(solution)/shard_map/ppermute | solution.py:30
  192.2 1.5 collective-permute-done.20
  193.7 5.7 %collective-permute-start.28 = (f32[1,8,64]{2,1,0:T(8,128)S(1)}, f32[1,8,64]{2,1,0:T(8,128)S(1)}, u32[]{:S(2)}, u32[]{:S(2)}) collective-permute-start(f32[1,8,64]{2,1,0:T(8,128)S(1)} %collective-permute-done.27), channel_id=1, source_target_pairs={{2,0},{4,2},{6,4},{8,6},{10,8},{12,10},{14,12},{16,14},{18,16},{20... | collective-permute-start | bytes 6152 | tf_op jit(solution)/shard_map/ppermute | solution.py:30
  199.4 1.5 collective-permute-done.21
  201.0 0.6 gather_fusion
  201.9 1.3 collective-permute-start.29
  203.2 1.8 collective-permute-done.29
  205.0 2.1 collective-permute-start.30
  207.1 0.8 collective-permute-done.30
  208.0 1.3 collective-permute-start.31
  209.3 1.8 collective-permute-done.31
  211.1 2.1 collective-permute-start.32
  213.2 1.0 slice.689
  214.2 0.7 slice.719
  214.8 0.6 slice.741
  216.0 0.7 copy.57
  (227 shorter events, 8.6 us)
Async XLA Ops:
  0.6 40.6 %copy-start = (f32[8,64,512]{2,1,0:T(8,128)S(1)}, f32[8,64,512]{2,1,0:T(8,128)}, u32[]{:S(2)}) copy-start(f32[8,64,512]{2,1,0:T(8,128)} %param.1) | copy-start | bytes 3145732
  43.1 16.6 %collective-permute-start.1 = (f32[2,8,4,256]{3,2,1,0:T(4,128)S(1)}, f32[2,8,4,256]{3,2,1,0:T(4,128)S(1)}, u32[]{:S(2)}, u32[]{:S(2)}) collective-permute-start(f32[2,8,4,256]{3,2,1,0:T(4,128)S(1)} %get-tuple-element.41), channel_id=1, source_target_pairs={{1,0},{3,2},{5,4},{7,6},{9,8},{11,10},{13,12},{15,14},{17,16},{19,... | collective-permute-start | bytes 196616 | tf_op jit(solution)/shard_map/ppermute | solution.py:47
  44.4 15.3 %collective-permute-start = (f32[2,8,4,256]{3,2,1,0:T(4,128)S(1)}, f32[2,8,4,256]{3,2,1,0:T(4,128)S(1)}, u32[]{:S(2)}, u32[]{:S(2)}) collective-permute-start(f32[2,8,4,256]{3,2,1,0:T(4,128)S(1)} %get-tuple-element.40), channel_id=1, source_target_pairs={{0,1},{2,3},{4,5},{6,7},{8,9},{10,11},{12,13},{14,15},{16,17},{18,... | collective-permute-start | bytes 196616 | tf_op jit(solution)/shard_map/ppermute | solution.py:45
  57.0 2.8 %copy-start.6 = (f32[128,64]{0,1:T(8,128)}, f32[128,64]{0,1:T(8,128)S(1)}, u32[]{:S(2)}) copy-start(f32[128,64]{0,1:T(8,128)S(1)} %fusion.97) | copy-start | bytes 98308
  57.3 2.5 %copy-start.2 = (f32[128,64]{0,1:T(8,128)}, f32[128,64]{0,1:T(8,128)S(1)}, u32[]{:S(2)}) copy-start(f32[128,64]{0,1:T(8,128)S(1)} %fusion.99) | copy-start | bytes 98308
  62.8 1.1 copy-start.1
  64.6 1.5 copy-start.4
  64.6 1.5 copy-start.5
  64.8 17.6 %collective-permute-start.3 = (f32[2,2,4,32,256]{4,3,2,1,0:T(8,128)S(1)}, f32[2,2,4,32,256]{4,3,2,1,0:T(8,128)S(1)}, u32[]{:S(2)}, u32[]{:S(2)}) collective-permute-start(f32[2,2,4,32,256]{4,3,2,1,0:T(8,128)S(1)} %get-tuple-element.38), channel_id=1, source_target_pairs={{2,0},{4,2},{6,4},{8,6},{10,8},{12,10},{14,12},{16,14},{18,16},{20... | collective-permute-start | bytes 1572872 | tf_op jit(solution)/shard_map/ppermute | solution.py:47
  66.2 27.2 %collective-permute-start.2 = (f32[2,2,4,32,256]{4,3,2,1,0:T(8,128)S(1)}, f32[2,2,4,32,256]{4,3,2,1,0:T(8,128)S(1)}, u32[]{:S(2)}, u32[]{:S(2)}) collective-permute-start(f32[2,2,4,32,256]{4,3,2,1,0:T(8,128)S(1)} %get-tuple-element.37), channel_id=1, source_target_pairs={{0,2},{2,4},{4,6},{6,8},{8,10},{10,12},{12,14},{14,16},{16,18},{18... | collective-permute-start | bytes 1572872 | tf_op jit(solution)/shard_map/ppermute | solution.py:45
  95.6 1.8 copy-start.3
  95.6 1.8 copy-start.7
  95.6 1.8 copy-start.8
  96.0 4.5 %collective-permute-start.5 = (f32[2,4,4,128]{3,2,1,0:T(4,128)S(1)}, f32[2,4,4,128]{3,2,1,0:T(4,128)S(1)}, u32[]{:S(2)}, u32[]{:S(2)}) collective-permute-start(f32[2,4,4,128]{3,2,1,0:T(4,128)S(1)} %get-tuple-element.47), channel_id=1, source_target_pairs={{1,0},{3,2},{5,4},{7,6},{9,8},{11,10},{13,12},{15,14},{17,16},{19,... | collective-permute-start | bytes 49160 | tf_op jit(solution)/shard_map/ppermute | solution.py:47
  97.5 3.9 %collective-permute-start.4 = (f32[2,4,4,128]{3,2,1,0:T(4,128)S(1)}, f32[2,4,4,128]{3,2,1,0:T(4,128)S(1)}, u32[]{:S(2)}, u32[]{:S(2)}) collective-permute-start(f32[2,4,4,128]{3,2,1,0:T(4,128)S(1)} %get-tuple-element.46), channel_id=1, source_target_pairs={{0,1},{2,3},{4,5},{6,7},{8,9},{10,11},{12,13},{14,15},{16,17},{18,... | collective-permute-start | bytes 49160 | tf_op jit(solution)/shard_map/ppermute | solution.py:45
  101.8 8.4 %collective-permute-start.6 = (f32[2,2,4,16,128]{4,3,2,1,0:T(8,128)S(1)}, f32[2,2,4,16,128]{4,3,2,1,0:T(8,128)S(1)}, u32[]{:S(2)}, u32[]{:S(2)}) collective-permute-start(f32[2,2,4,16,128]{4,3,2,1,0:T(8,128)S(1)} %pad_maximum_fusion.9), channel_id=1, source_target_pairs={{2,0},{4,2},{6,4},{8,6},{10,8},{12,10},{14,12},{16,14},{18,16},{20... | collective-permute-start | bytes 393224 | tf_op jit(solution)/shard_map/ppermute | solution.py:47
  103.1 9.1 %collective-permute-start.7 = (f32[2,2,4,16,128]{4,3,2,1,0:T(8,128)S(1)}, f32[2,2,4,16,128]{4,3,2,1,0:T(8,128)S(1)}, u32[]{:S(2)}, u32[]{:S(2)}) collective-permute-start(f32[2,2,4,16,128]{4,3,2,1,0:T(8,128)S(1)} %pad_maximum_fusion.9), channel_id=1, source_target_pairs={{0,2},{2,4},{4,6},{6,8},{8,10},{10,12},{12,14},{14,16},{16,18},{18... | collective-permute-start | bytes 393224 | tf_op jit(solution)/shard_map/ppermute | solution.py:45
  113.0 4.4 %collective-permute-start.9 = (f32[2,2,4,64]{3,2,1,0:T(4,128)S(1)}, f32[2,2,4,64]{3,2,1,0:T(4,128)S(1)}, u32[]{:S(2)}, u32[]{:S(2)}) collective-permute-start(f32[2,2,4,64]{3,2,1,0:T(4,128)S(1)} %get-tuple-element.51), channel_id=1, source_target_pairs={{1,0},{3,2},{5,4},{7,6},{9,8},{11,10},{13,12},{15,14},{17,16},{19,... | collective-permute-start | bytes 12296 | tf_op jit(solution)/shard_map/ppermute | solution.py:47
  114.4 3.8 %collective-permute-start.8 = (f32[2,2,4,64]{3,2,1,0:T(4,128)S(1)}, f32[2,2,4,64]{3,2,1,0:T(4,128)S(1)}, u32[]{:S(2)}, u32[]{:S(2)}) collective-permute-start(f32[2,2,4,64]{3,2,1,0:T(4,128)S(1)} %get-tuple-element.50), channel_id=1, source_target_pairs={{0,1},{2,3},{4,5},{6,7},{8,9},{10,11},{12,13},{14,15},{16,17},{18,... | collective-permute-start | bytes 12296 | tf_op jit(solution)/shard_map/ppermute | solution.py:45
  118.6 6.1 %collective-permute-start.10 = (f32[2,2,1,8,64]{4,3,1,0,2:T(8,128)S(1)}, f32[2,2,1,8,64]{4,3,1,0,2:T(8,128)S(1)}, u32[]{:S(2)}, u32[]{:S(2)}) collective-permute-start(f32[2,2,1,8,64]{4,3,1,0,2:T(8,128)S(1)} %maximum_bitcast_fusion.8), channel_id=1, source_target_pairs={{2,0},{4,2},{6,4},{8,6},{10,8},{12,10},{14,12},{16,14},{18,16},{20... | collective-permute-start | bytes 24584 | tf_op jit(solution)/shard_map/ppermute | solution.py:57
  124.7 6.3 %collective-permute-start.11 = (f32[2,2,1,8,64]{4,3,1,0,2:T(8,128)S(1)}, f32[2,2,1,8,64]{4,3,1,0,2:T(8,128)S(1)}, u32[]{:S(2)}, u32[]{:S(2)}) collective-permute-start(f32[2,2,1,8,64]{4,3,1,0,2:T(8,128)S(1)} %bitcast.246), channel_id=1, source_target_pairs={{0,2},{2,4},{4,6},{6,8},{8,10},{10,12},{12,14},{14,16},{16,18},{18... | collective-permute-start | bytes 24584 | tf_op jit(solution)/shard_map/ppermute | solution.py:57
  131.0 5.9 %collective-permute-start.12 = (f32[2,2,1,8,64]{4,3,1,0,2:T(8,128)S(1)}, f32[2,2,1,8,64]{4,3,1,0,2:T(8,128)S(1)}, u32[]{:S(2)}, u32[]{:S(2)}) collective-permute-start(f32[2,2,1,8,64]{4,3,1,0,2:T(8,128)S(1)} %fusion.123), channel_id=1, source_target_pairs={{2,0},{4,2},{6,4},{8,6},{10,8},{12,10},{14,12},{16,14},{18,16},{20... | collective-permute-start | bytes 24584 | tf_op jit(solution)/shard_map/ppermute | solution.py:57
  136.9 6.3 %collective-permute-start.13 = (f32[2,2,1,8,64]{4,3,1,0,2:T(8,128)S(1)}, f32[2,2,1,8,64]{4,3,1,0,2:T(8,128)S(1)}, u32[]{:S(2)}, u32[]{:S(2)}) collective-permute-start(f32[2,2,1,8,64]{4,3,1,0,2:T(8,128)S(1)} %bitcast.255), channel_id=1, source_target_pairs={{0,2},{2,4},{4,6},{6,8},{8,10},{10,12},{12,14},{14,16},{16,18},{18... | collective-permute-start | bytes 24584 | tf_op jit(solution)/shard_map/ppermute | solution.py:57
  143.2 7.3 %collective-permute-start.14 = (f32[1,8,64]{2,1,0:T(8,128)S(1)}, f32[1,8,64]{2,1,0:T(8,128)S(1)}, u32[]{:S(2)}, u32[]{:S(2)}) collective-permute-start(f32[1,8,64]{2,1,0:T(8,128)S(1)} %slice_bitcast_fusion.4), channel_id=1, source_target_pairs={{0,2},{2,4},{4,6},{6,8},{8,10},{10,12},{12,14},{14,16},{16,18},{18... | collective-permute-start | bytes 6152 | tf_op jit(solution)/shard_map/ppermute | solution.py:28
  150.4 7.2 %collective-permute-start.15 = (f32[1,8,64]{2,1,0:T(8,128)S(1)}, f32[1,8,64]{2,1,0:T(8,128)S(1)}, u32[]{:S(2)}, u32[]{:S(2)}) collective-permute-start(f32[1,8,64]{2,1,0:T(8,128)S(1)} %collective-permute-done.14), channel_id=1, source_target_pairs={{0,2},{2,4},{4,6},{6,8},{8,10},{10,12},{12,14},{14,16},{16,18},{18... | collective-permute-start | bytes 6152 | tf_op jit(solution)/shard_map/ppermute | solution.py:28
  150.5 7.2 %collective-permute-start.22 = (f32[1,8,64]{2,1,0:T(8,128)S(1)}, f32[1,8,64]{2,1,0:T(8,128)S(1)}, u32[]{:S(2)}, u32[]{:S(2)}) collective-permute-start(f32[1,8,64]{2,1,0:T(8,128)S(1)} %slice_bitcast_fusion.4), channel_id=1, source_target_pairs={{2,0},{4,2},{6,4},{8,6},{10,8},{12,10},{14,12},{16,14},{18,16},{20... | collective-permute-start | bytes 6152 | tf_op jit(solution)/shard_map/ppermute | solution.py:30
  157.6 7.2 %collective-permute-start.16 = (f32[1,8,64]{2,1,0:T(8,128)S(1)}, f32[1,8,64]{2,1,0:T(8,128)S(1)}, u32[]{:S(2)}, u32[]{:S(2)}) collective-permute-start(f32[1,8,64]{2,1,0:T(8,128)S(1)} %collective-permute-done.15), channel_id=1, source_target_pairs={{0,2},{2,4},{4,6},{6,8},{8,10},{10,12},{12,14},{14,16},{16,18},{18... | collective-permute-start | bytes 6152 | tf_op jit(solution)/shard_map/ppermute | solution.py:28
  157.7 7.2 %collective-permute-start.23 = (f32[1,8,64]{2,1,0:T(8,128)S(1)}, f32[1,8,64]{2,1,0:T(8,128)S(1)}, u32[]{:S(2)}, u32[]{:S(2)}) collective-permute-start(f32[1,8,64]{2,1,0:T(8,128)S(1)} %collective-permute-done.22), channel_id=1, source_target_pairs={{2,0},{4,2},{6,4},{8,6},{10,8},{12,10},{14,12},{16,14},{18,16},{20... | collective-permute-start | bytes 6152 | tf_op jit(solution)/shard_map/ppermute | solution.py:30
  164.8 7.2 %collective-permute-start.17 = (f32[1,8,64]{2,1,0:T(8,128)S(1)}, f32[1,8,64]{2,1,0:T(8,128)S(1)}, u32[]{:S(2)}, u32[]{:S(2)}) collective-permute-start(f32[1,8,64]{2,1,0:T(8,128)S(1)} %collective-permute-done.16), channel_id=1, source_target_pairs={{0,2},{2,4},{4,6},{6,8},{8,10},{10,12},{12,14},{14,16},{16,18},{18... | collective-permute-start | bytes 6152 | tf_op jit(solution)/shard_map/ppermute | solution.py:28
  164.9 7.2 %collective-permute-start.24 = (f32[1,8,64]{2,1,0:T(8,128)S(1)}, f32[1,8,64]{2,1,0:T(8,128)S(1)}, u32[]{:S(2)}, u32[]{:S(2)}) collective-permute-start(f32[1,8,64]{2,1,0:T(8,128)S(1)} %collective-permute-done.23), channel_id=1, source_target_pairs={{2,0},{4,2},{6,4},{8,6},{10,8},{12,10},{14,12},{16,14},{18,16},{20... | collective-permute-start | bytes 6152 | tf_op jit(solution)/shard_map/ppermute | solution.py:30
  172.0 7.2 %collective-permute-start.18 = (f32[1,8,64]{2,1,0:T(8,128)S(1)}, f32[1,8,64]{2,1,0:T(8,128)S(1)}, u32[]{:S(2)}, u32[]{:S(2)}) collective-permute-start(f32[1,8,64]{2,1,0:T(8,128)S(1)} %collective-permute-done.17), channel_id=1, source_target_pairs={{0,2},{2,4},{4,6},{6,8},{8,10},{10,12},{12,14},{14,16},{16,18},{18... | collective-permute-start | bytes 6152 | tf_op jit(solution)/shard_map/ppermute | solution.py:28
  172.1 7.2 %collective-permute-start.25 = (f32[1,8,64]{2,1,0:T(8,128)S(1)}, f32[1,8,64]{2,1,0:T(8,128)S(1)}, u32[]{:S(2)}, u32[]{:S(2)}) collective-permute-start(f32[1,8,64]{2,1,0:T(8,128)S(1)} %collective-permute-done.24), channel_id=1, source_target_pairs={{2,0},{4,2},{6,4},{8,6},{10,8},{12,10},{14,12},{16,14},{18,16},{20... | collective-permute-start | bytes 6152 | tf_op jit(solution)/shard_map/ppermute | solution.py:30
  179.2 7.2 %collective-permute-start.19 = (f32[1,8,64]{2,1,0:T(8,128)S(1)}, f32[1,8,64]{2,1,0:T(8,128)S(1)}, u32[]{:S(2)}, u32[]{:S(2)}) collective-permute-start(f32[1,8,64]{2,1,0:T(8,128)S(1)} %collective-permute-done.18), channel_id=1, source_target_pairs={{0,2},{2,4},{4,6},{6,8},{8,10},{10,12},{12,14},{14,16},{16,18},{18... | collective-permute-start | bytes 6152 | tf_op jit(solution)/shard_map/ppermute | solution.py:28
  179.3 7.2 %collective-permute-start.26 = (f32[1,8,64]{2,1,0:T(8,128)S(1)}, f32[1,8,64]{2,1,0:T(8,128)S(1)}, u32[]{:S(2)}, u32[]{:S(2)}) collective-permute-start(f32[1,8,64]{2,1,0:T(8,128)S(1)} %collective-permute-done.25), channel_id=1, source_target_pairs={{2,0},{4,2},{6,4},{8,6},{10,8},{12,10},{14,12},{16,14},{18,16},{20... | collective-permute-start | bytes 6152 | tf_op jit(solution)/shard_map/ppermute | solution.py:30
  186.4 7.2 %collective-permute-start.20 = (f32[1,8,64]{2,1,0:T(8,128)S(1)}, f32[1,8,64]{2,1,0:T(8,128)S(1)}, u32[]{:S(2)}, u32[]{:S(2)}) collective-permute-start(f32[1,8,64]{2,1,0:T(8,128)S(1)} %collective-permute-done.19), channel_id=1, source_target_pairs={{0,2},{2,4},{4,6},{6,8},{8,10},{10,12},{12,14},{14,16},{16,18},{18... | collective-permute-start | bytes 6152 | tf_op jit(solution)/shard_map/ppermute | solution.py:28
  186.5 7.2 %collective-permute-start.27 = (f32[1,8,64]{2,1,0:T(8,128)S(1)}, f32[1,8,64]{2,1,0:T(8,128)S(1)}, u32[]{:S(2)}, u32[]{:S(2)}) collective-permute-start(f32[1,8,64]{2,1,0:T(8,128)S(1)} %collective-permute-done.26), channel_id=1, source_target_pairs={{2,0},{4,2},{6,4},{8,6},{10,8},{12,10},{14,12},{16,14},{18,16},{20... | collective-permute-start | bytes 6152 | tf_op jit(solution)/shard_map/ppermute | solution.py:30
  193.6 7.2 %collective-permute-start.21 = (f32[1,8,64]{2,1,0:T(8,128)S(1)}, f32[1,8,64]{2,1,0:T(8,128)S(1)}, u32[]{:S(2)}, u32[]{:S(2)}) collective-permute-start(f32[1,8,64]{2,1,0:T(8,128)S(1)} %collective-permute-done.20), channel_id=1, source_target_pairs={{0,2},{2,4},{4,6},{6,8},{8,10},{10,12},{12,14},{14,16},{16,18},{18... | collective-permute-start | bytes 6152 | tf_op jit(solution)/shard_map/ppermute | solution.py:28
  193.7 7.3 %collective-permute-start.28 = (f32[1,8,64]{2,1,0:T(8,128)S(1)}, f32[1,8,64]{2,1,0:T(8,128)S(1)}, u32[]{:S(2)}, u32[]{:S(2)}) collective-permute-start(f32[1,8,64]{2,1,0:T(8,128)S(1)} %collective-permute-done.27), channel_id=1, source_target_pairs={{2,0},{4,2},{6,4},{8,6},{10,8},{12,10},{14,12},{16,14},{18,16},{20... | collective-permute-start | bytes 6152 | tf_op jit(solution)/shard_map/ppermute | solution.py:30
  201.9 3.1 %collective-permute-start.29 = (f32[2,16,1,32]{3,1,2,0:T(8,128)S(1)}, f32[2,16,1,32]{3,1,2,0:T(8,128)S(1)}, u32[]{:S(2)}, u32[]{:S(2)}) collective-permute-start(f32[2,16,1,32]{3,1,2,0:T(8,128)S(1)} %slice.753), channel_id=1, source_target_pairs={{1,0},{3,2},{5,4},{7,6},{9,8},{11,10},{13,12},{15,14},{17,16},{19,... | collective-permute-start | bytes 12296 | tf_op jit(solution)/shard_map/ppermute | solution.py:57
  205.0 2.9 %collective-permute-start.30 = (f32[2,16,1,32]{3,1,2,0:T(8,128)S(1)}, f32[2,16,1,32]{3,1,2,0:T(8,128)S(1)}, u32[]{:S(2)}, u32[]{:S(2)}) collective-permute-start(f32[2,16,1,32]{3,1,2,0:T(8,128)S(1)} %slice.755), channel_id=1, source_target_pairs={{0,1},{2,3},{4,5},{6,7},{8,9},{10,11},{12,13},{14,15},{16,17},{18,... | collective-permute-start | bytes 12296 | tf_op jit(solution)/shard_map/ppermute | solution.py:57
  208.0 3.1 %collective-permute-start.31 = (f32[2,16,1,32]{3,1,2,0:T(8,128)S(1)}, f32[2,16,1,32]{3,1,2,0:T(8,128)S(1)}, u32[]{:S(2)}, u32[]{:S(2)}) collective-permute-start(f32[2,16,1,32]{3,1,2,0:T(8,128)S(1)} %slice.759), channel_id=1, source_target_pairs={{1,0},{3,2},{5,4},{7,6},{9,8},{11,10},{13,12},{15,14},{17,16},{19,... | collective-permute-start | bytes 12296 | tf_op jit(solution)/shard_map/ppermute | solution.py:57
  211.1 4.3 %collective-permute-start.32 = (f32[2,16,1,32]{3,1,2,0:T(8,128)S(1)}, f32[2,16,1,32]{3,1,2,0:T(8,128)S(1)}, u32[]{:S(2)}, u32[]{:S(2)}) collective-permute-start(f32[2,16,1,32]{3,1,2,0:T(8,128)S(1)} %slice.761), channel_id=1, source_target_pairs={{0,1},{2,3},{4,5},{6,7},{8,9},{10,11},{12,13},{14,15},{16,17},{18,... | collective-permute-start | bytes 12296 | tf_op jit(solution)/shard_map/ppermute | solution.py:57
